TPU v7x, 32 devices: a whole 2x2x4 slice. The times are simulated.
32 devices in a mesh: probe: 4 (over z), gx: 4 (over x, core), gy: 2 (over y).
Axes of the slice: x: 2, y: 2, z: 4, core: 2. Of those that a mesh axis runs over, the one named last changes fastest.
Arguments:
- wave_prev: float32 [4, 128, 256, 256], P('probe', 'gx', 'gy'), may hold values from -6 to 6
- wave_cur: float32 [4, 128, 256, 256], P('probe', 'gx', 'gy'), may hold values from -6 to 6
- courant: float32 [128, 256, 256], P('gx', 'gy'), may hold values from 0.02 to 0.16
- perturb: float32 [4, 128, 256, 256], P('probe', 'gx', 'gy'), may hold values from -4 to 4
- snapshots: bfloat16 [8, 128, 256, 256], P('probe', 'gx', 'gy'), may hold values from -6 to 6
- step_slots: int32 [6], replicated, may hold values from 0 to 7, as said below
- precond: float32 [256], replicated, may hold values from 0.5 to 2
- probe_ids: int32 [4], P('probe'), may hold values from 0 to 255, as said below
Outputs:
- earlier: float32 [4, 128, 256, 256], P('probe', 'gx', 'gy')
- latest: float32 [4, 128, 256, 256], P('probe', 'gx', 'gy')
Inputs may be any that keep to these rules, and one draw needn't show every extreme that they name: `step_slots`: distinct slots; 0 and 7 are always among them. `probe_ids`: distinct indices; 0 and 255 are always among them.
All inputs are finite; a program needn't handle non-finite values.
Results may differ from a plain program's by a relative error of at most 0.0003.
Values may be sent and summed in bfloat16 or wider, within the bound.
A program may use at most 192 MiB of HBM per device.

v0:
```python
import jax
import jax.numpy as jnp
from jax import lax
from jax.sharding import PartitionSpec as P

STEPS = 4
COEFFS = (-205.0 / 72.0, 8.0 / 5.0, -1.0 / 5.0, 8.0 / 315.0, -1.0 / 560.0)


def spread(value, axis, source):
    kept = jnp.where(lax.axis_index(axis) == source, value, 0).astype(value.dtype)
    return lax.psum(kept, axis)


def with_halo(block, sides, width):
    for axis, dim in sides:
        count = lax.axis_size(axis)
        forward = [(i, i + 1) for i in range(count - 1)]
        backward = [(target, source) for source, target in forward]
        low = lax.ppermute(
            lax.slice_in_dim(block, block.shape[dim] - width, None, axis=dim), axis, forward
        )
        high = lax.ppermute(lax.slice_in_dim(block, 0, width, axis=dim), axis, backward)
        block = jnp.concatenate([low, block, high], axis=dim)
    return block


def stencil(padded, field):
    extent_x = field.shape[1]
    extent_y = field.shape[2]
    extent_z = field.shape[3]
    total = 3.0 * COEFFS[0] * field
    for offset in range(1, 5):
        factor = COEFFS[offset]
        along = padded[:, 4 + offset : 4 + offset + extent_x, 4 : 4 + extent_y, 4 : 4 + extent_z]
        along = (
            along
            + padded[:, 4 - offset : 4 - offset + extent_x, 4 : 4 + extent_y, 4 : 4 + extent_z]
        )
        along = (
            along
            + padded[:, 4 : 4 + extent_x, 4 + offset : 4 + offset + extent_y, 4 : 4 + extent_z]
        )
        along = (
            along
            + padded[:, 4 : 4 + extent_x, 4 - offset : 4 - offset + extent_y, 4 : 4 + extent_z]
        )
        along = (
            along
            + padded[:, 4 : 4 + extent_x, 4 : 4 + extent_y, 4 + offset : 4 + offset + extent_z]
        )
        along = (
            along
            + padded[:, 4 : 4 + extent_x, 4 : 4 + extent_y, 4 - offset : 4 - offset + extent_z]
        )
        total = total + factor * along
    return total


def shards(wave_prev, wave_cur, courant, perturb, snapshots, step_slots, precond, probe_ids):
    table = jnp.arange(precond.shape[0], dtype=jnp.int32)
    matches = (probe_ids[:, None] == table[None, :]).astype(jnp.float32)
    weight = jnp.sum(matches * precond[None, :], axis=1)
    scaled = weight[:, None, None, None] * perturb
    slot_dev = snapshots.shape[0]

    def fetch(position):
        wanted = step_slots[position]
        owner = wanted // slot_dev
        holding = lax.dynamic_index_in_dim(snapshots, wanted % slot_dev, 0, keepdims=False)
        return spread(holding, "probe", owner).astype(jnp.float32)

    frames = [fetch(0), fetch(1)]
    previous = wave_prev
    current = wave_cur
    for index in range(STEPS):
        frames.append(fetch(index + 2))
        source = frames[index + 2] - 2.0 * frames[index + 1] + frames[index]
        widened = with_halo(current, (("gx", 1), ("gy", 2)), 4)
        padded = jnp.pad(widened, ((0, 0), (0, 0), (0, 0), (4, 4)))
        laplace = stencil(padded, current)
        following = 2.0 * current - previous + courant[None] * laplace - scaled * source[None]
        previous = current
        current = following
    return (previous, current)


def solution(mesh):
    placed = (
        P("probe", "gx", "gy", None),
        P("probe", "gx", "gy", None),
        P("gx", "gy", None),
        P("probe", "gx", "gy", None),
        P("probe", "gx", "gy", None),
        P(),
        P(),
        P("probe"),
    )
    return jax.shard_map(
        shards,
        mesh=mesh,
        in_specs=placed,
        out_specs=(P("probe", "gx", "gy", None), P("probe", "gx", "gy", None)),
        check_vma=False,
    )
```

profile of v0, /device:TPU:6, one launch (start us, length us, event | category | flops | bytes accessed | tf_op | source)
XLA Modules:
  0.0 834.7 jit_solution(7365499890127130381)
XLA Ops:
  23.9 9.7 %select_bitcast_fusion = (bf16[32,128,256]{2,1,0:T(8,128)(2,1)}, bf16[32,128,256]{2,1,0:T(8,128)(2,1)}, bf16[32,128,256]{2,1,0:T(8,128)(2,1)}, bf16[32,128,256]{...) fusion(bf16[2,32,128,256]{3,2,1,0:T(8,128)(2,1)} %param.12, s32[]{:T(128)S(6)} %select_n.154, ...), kind=kLoop, calls=%fused_computation.247 | loop fusion | flops 6291456 | bytes 25165854 | tf_op jit(solution)/shard_map/jit(_where)/select_n | solution.py:11
  36.8 3.6 collective-permute-start
  40.5 4.9 collective-permute-done.1
  46.3 7.0 constant_dynamic-update-slice_fusion.1
  54.2 2.4 collective-permute-start.2
  59.5 4.4 collective-permute-done.3
  63.9 5.8 select_maximum_fusion.12
  69.6 394.8 %all-reduce.7.cloned.1.call-done = (bf16[32,128,256]{2,1,0:T(8,128)(2,1)}, bf16[32,128,256]{2,1,0:T(8,128)(2,1)}, bf16[32,128,256]{2,1,0:T(8,128)(2,1)}, bf16[32...) async-done(((bf16[32,128,256]{2,1,0:T(8,128)(2,1)}, bf16[32,128,256]{2,1,0:T(8,128)(2,1)}, bf16[32,128,256]{2,1,0:T(8,128)(2,1)}, ...) | async-done | bytes 12582928 | tf_op jit(solution)/shard_map/psum | solution.py:12
  464.5 55.3 %fusion.103 = f32[1,32,128,256]{3,2,1,0:T(8,128)S(1)} fusion(f32[1,40,128,256]{3,2,1,0:T(8,128)} %copy-done.3, bf16[32,128,256]{2,1,0:T(8,128)(2,1)} %get-tuple-element.2, bf16[32,128,256]{2,1,0:T(8,128)(2,1)} %get-tuple-element.3, f32[1,40,4,256]{3,2,1,0:T(4,128)S(1)} %collective-permute-done.3, f32[1,40,4,256]{3,2,1,0:T(4,128)S(1)} %collective-permute-done.2, ...), kind=kLoop, calls=%fused_computation.183 | loop fusion | flops 52428800 | bytes 99942400 | tf_op jit(solution)/shard_map/sub | solution.py:82
  521.8 2.4 collective-permute-start.5
  524.2 4.2 collective-permute-done.4
  528.4 3.8 collective-permute-done.5
  532.3 2.5 collective-permute-start.6
  537.6 4.4 collective-permute-done.7
  542.0 4.9 pad_maximum_fusion
  546.9 8.7 %select_maximum_fusion.8 = f32[1,40,136,264]{3,2,1,0:T(8,128)} fusion(f32[1,40,4,256]{3,2,1,0:T(4,128)S(1)} %collective-permute-done.6, f32[1,40,4,256]{3,2,1,0:T(4,128)S(1)} %collective-permute-done.7, f32[1,4,128,256]{3,2,1,0:T(8,128)S(1)} %collective-permute-done.4, f32[1,32,128,256]{3,2,1,0:T(8,128)S(1)} %fusion.103, ...), kind=kLoop, calls=%fused_computation.16 | loop fusion | flops 17233920 | bytes 11315200 | tf_op jit(solution)/shard_map/concatenate | solution.py:24
  555.6 66.3 %fusion.74 = f32[1,32,128,256]{3,2,1,0:T(8,128)} fusion(f32[1,32,128,256]{3,2,1,0:T(8,128)} %copy-done, bf16[32,128,256]{2,1,0:T(8,128)(2,1)} %get-tuple-element.2, bf16[32,128,256]{2,1,0:T(8,128)(2,1)S(1)} %copy-done.4, bf16[32,128,256]{2,1,0:T(8,128)(2,1)} %get-tuple-element.5, f32[1,4,128,256]{3,2,1,0:T(8,128)S(1)} %collective-permute-done.5, ...), kind=kLoop, calls=%fused_computation.154 | loop fusion | flops 52428800 | bytes 95420416 | tf_op jit(solution)/shard_map/sub | solution.py:82
  623.3 2.1 collective-permute-start.8
  625.4 2.4 collective-permute-start.9
  627.8 4.2 collective-permute-done.8
  632.1 3.8 collective-permute-done.9
  641.3 4.4 collective-permute-done.11
  645.7 4.9 pad_maximum_fusion.1
  650.6 8.7 %select_maximum_fusion.4 = f32[1,40,136,264]{3,2,1,0:T(8,128)} fusion(f32[1,40,4,256]{3,2,1,0:T(4,128)S(1)} %collective-permute-done.10, f32[1,40,4,256]{3,2,1,0:T(4,128)S(1)} %collective-permute-done.11, f32[1,4,128,256]{3,2,1,0:T(8,128)S(1)} %collective-permute-done.8, f32[1,32,128,256]{3,2,1,0:T(8,128)S(1)} %copy-done.1, ...), kind=kLoop, calls=%fused_computation.12 | loop fusion | flops 17233920 | bytes 11315200 | tf_op jit(solution)/shard_map/concatenate | solution.py:24
  659.2 65.8 %fusion.43 = f32[1,32,128,256]{3,2,1,0:T(8,128)} fusion(f32[1,32,128,256]{3,2,1,0:T(8,128)} %fusion.74, bf16[32,128,256]{2,1,0:T(8,128)(2,1)S(1)} %copy-done.4, bf16[32,128,256]{2,1,0:T(8,128)(2,1)} %get-tuple-element.6, bf16[32,128,256]{2,1,0:T(8,128)(2,1)} %get-tuple-element.5, f32[1,4,128,256]{3,2,1,0:T(8,128)S(1)} %collective-permute-done.9, ...), kind=kLoop, calls=%fused_computation.123 | loop fusion | flops 52428800 | bytes 95420416 | tf_op jit(solution)/shard_map/sub | solution.py:82
  728.5 2.4 collective-permute-start.13
  731.0 4.2 collective-permute-done.12
  735.2 3.8 collective-permute-done.13
  744.4 4.4 collective-permute-done.15
  748.8 4.9 pad_maximum_fusion.2
  753.7 8.7 %select_maximum_fusion = f32[1,40,136,264]{3,2,1,0:T(8,128)} fusion(f32[1,40,4,256]{3,2,1,0:T(4,128)S(1)} %collective-permute-done.14, f32[1,40,4,256]{3,2,1,0:T(4,128)S(1)} %collective-permute-done.15, f32[1,4,128,256]{3,2,1,0:T(8,128)S(1)} %collective-permute-done.12, f32[1,32,128,256]{3,2,1,0:T(8,128)S(1)} %copy-done.2, ...), kind=kLoop, calls=%fused_computation.8 | loop fusion | flops 17233920 | bytes 11315200 | tf_op jit(solution)/shard_map/concatenate | solution.py:24
  762.3 65.5 %fusion.12 = f32[1,32,128,256]{3,2,1,0:T(8,128)} fusion(f32[1,32,128,256]{3,2,1,0:T(8,128)} %fusion.43, bf16[32,128,256]{2,1,0:T(8,128)(2,1)S(1)} %copy-done.5, bf16[32,128,256]{2,1,0:T(8,128)(2,1)} %get-tuple-element.6, f32[1,4,128,256]{3,2,1,0:T(8,128)S(1)} %collective-permute-done.13, f32[1,4,128,256]{3,2,1,0:T(8,128)S(1)} %collective-permute-done.12, ...), kind=kLoop, calls=%fused_computation.92 | loop fusion | flops 52428800 | bytes 95420416 | tf_op jit(solution)/shard_map/sub | solution.py:82
  (42 shorter events, 29.2 us)
Async XLA Ops:
  7.2 457.3 %all-reduce.7.cloned.1.call-start = ((), (), s32[]{:S(2)}) async-start(), calls=%async_computation | async-start | bytes 25165824 | tf_op jit(solution)/shard_map/psum | solution.py:12
  34.9 10.5 %collective-permute-start.1 = (f32[1,4,128,256]{3,2,1,0:T(8,128)S(1)}, f32[1,4,128,256]{3,2,1,0:T(8,128)S(1)}, u32[]{:S(2)}, u32[]{:S(2)}) collective-permute-start(f32[1,4,128,256]{3,2,1,0:T(8,128)S(1)} %get-tuple-element.38), channel_id=1, source_target_pairs={{0,2},{2,4},{4,6},{1,3},{3,5},{5,7},{8,10},{10,12},{12,14},{9,11},... | collective-permute-start | bytes 1572872 | tf_op jit(solution)/shard_map/ppermute | solution.py:20
  36.8 16.5 %collective-permute-start = (f32[1,4,128,256]{3,2,1,0:T(8,128)S(1)}, f32[1,4,128,256]{3,2,1,0:T(8,128)S(1)}, u32[]{:S(2)}, u32[]{:S(2)}) collective-permute-start(f32[1,4,128,256]{3,2,1,0:T(8,128)S(1)} %get-tuple-element.37), channel_id=1, source_target_pairs={{2,0},{4,2},{6,4},{3,1},{5,3},{7,5},{10,8},{12,10},{14,12},{11,9},... | collective-permute-start | bytes 1572872 | tf_op jit(solution)/shard_map/ppermute | solution.py:23
  46.3 12.3 %copy-start.6 = (f32[256]{0:T(256)S(1)}, f32[256]{0:T(256)}, u32[]{:S(2)}) copy-start(f32[256]{0:T(256)} %param.14) | copy-start | bytes 3076
  54.2 9.7 %copy-start.3 = (f32[1,40,128,256]{3,2,1,0:T(8,128)}, f32[1,40,128,256]{3,2,1,0:T(8,128)S(1)}, u32[]{:S(2)}) copy-start(f32[1,40,128,256]{3,2,1,0:T(8,128)S(1)} %get-tuple-element.40) | copy-start | bytes 15728644
  54.2 5.2 collective-permute-start.2
  56.7 7.2 collective-permute-start.3
  519.7 27.2 %copy-start = (f32[1,32,128,256]{3,2,1,0:T(8,128)}, f32[1,32,128,256]{3,2,1,0:T(8,128)S(1)}, u32[]{:S(2)}) copy-start(f32[1,32,128,256]{3,2,1,0:T(8,128)S(1)} %fusion.103) | copy-start | bytes 12582916
  519.8 8.6 %collective-permute-start.4 = (f32[1,4,128,256]{3,2,1,0:T(8,128)S(1)}, f32[1,4,128,256]{3,2,1,0:T(8,128)S(1)}, u32[]{:S(2)}, u32[]{:S(2)}) collective-permute-start(f32[1,4,128,256]{3,2,1,0:T(8,128)S(1)} %get-tuple-element.26), channel_id=1, source_target_pairs={{2,0},{4,2},{6,4},{3,1},{5,3},{7,5},{10,8},{12,10},{14,12},{11,9},... | collective-permute-start | bytes 1572872 | tf_op jit(solution)/shard_map/ppermute | solution.py:23
  521.8 10.5 %collective-permute-start.5 = (f32[1,4,128,256]{3,2,1,0:T(8,128)S(1)}, f32[1,4,128,256]{3,2,1,0:T(8,128)S(1)}, u32[]{:S(2)}, u32[]{:S(2)}) collective-permute-start(f32[1,4,128,256]{3,2,1,0:T(8,128)S(1)} %get-tuple-element.27), channel_id=1, source_target_pairs={{0,2},{2,4},{4,6},{1,3},{3,5},{5,7},{8,10},{10,12},{12,14},{9,11},... | collective-permute-start | bytes 1572872 | tf_op jit(solution)/shard_map/ppermute | solution.py:20
  532.3 5.3 collective-permute-start.6
  534.8 7.2 collective-permute-start.7
  546.9 8.7 %copy-start.4 = (bf16[32,128,256]{2,1,0:T(8,128)(2,1)S(1)}, bf16[32,128,256]{2,1,0:T(8,128)(2,1)}, u32[]{:S(2)}) copy-start(bf16[32,128,256]{2,1,0:T(8,128)(2,1)} %get-tuple-element.3) | copy-start | bytes 6291460
  621.9 23.8 %copy-start.1 = (f32[1,32,128,256]{3,2,1,0:T(8,128)S(1)}, f32[1,32,128,256]{3,2,1,0:T(8,128)}, u32[]{:S(2)}) copy-start(f32[1,32,128,256]{3,2,1,0:T(8,128)} %fusion.74) | copy-start | bytes 12582916
  623.3 8.7 %collective-permute-start.8 = (f32[1,4,128,256]{3,2,1,0:T(8,128)S(1)}, f32[1,4,128,256]{3,2,1,0:T(8,128)S(1)}, u32[]{:S(2)}, u32[]{:S(2)}) collective-permute-start(f32[1,4,128,256]{3,2,1,0:T(8,128)S(1)} %get-tuple-element.24), channel_id=1, source_target_pairs={{2,0},{4,2},{6,4},{3,1},{5,3},{7,5},{10,8},{12,10},{14,12},{11,9},... | collective-permute-start | bytes 1572872 | tf_op jit(solution)/shard_map/ppermute | solution.py:23
  625.4 10.5 %collective-permute-start.9 = (f32[1,4,128,256]{3,2,1,0:T(8,128)S(1)}, f32[1,4,128,256]{3,2,1,0:T(8,128)S(1)}, u32[]{:S(2)}, u32[]{:S(2)}) collective-permute-start(f32[1,4,128,256]{3,2,1,0:T(8,128)S(1)} %get-tuple-element.25), channel_id=1, source_target_pairs={{0,2},{2,4},{4,6},{1,3},{3,5},{5,7},{8,10},{10,12},{12,14},{9,11},... | collective-permute-start | bytes 1572872 | tf_op jit(solution)/shard_map/ppermute | solution.py:20
  637.0 4.3 collective-permute-start.10
  638.4 7.2 collective-permute-start.11
  725.0 23.8 %copy-start.2 = (f32[1,32,128,256]{3,2,1,0:T(8,128)S(1)}, f32[1,32,128,256]{3,2,1,0:T(8,128)}, u32[]{:S(2)}) copy-start(f32[1,32,128,256]{3,2,1,0:T(8,128)} %fusion.43) | copy-start | bytes 12582916
  726.5 8.7 %collective-permute-start.12 = (f32[1,4,128,256]{3,2,1,0:T(8,128)S(1)}, f32[1,4,128,256]{3,2,1,0:T(8,128)S(1)}, u32[]{:S(2)}, u32[]{:S(2)}) collective-permute-start(f32[1,4,128,256]{3,2,1,0:T(8,128)S(1)} %get-tuple-element.22), channel_id=1, source_target_pairs={{2,0},{4,2},{6,4},{3,1},{5,3},{7,5},{10,8},{12,10},{14,12},{11,9},... | collective-permute-start | bytes 1572872 | tf_op jit(solution)/shard_map/ppermute | solution.py:23
  728.5 10.5 %collective-permute-start.13 = (f32[1,4,128,256]{3,2,1,0:T(8,128)S(1)}, f32[1,4,128,256]{3,2,1,0:T(8,128)S(1)}, u32[]{:S(2)}, u32[]{:S(2)}) collective-permute-start(f32[1,4,128,256]{3,2,1,0:T(8,128)S(1)} %get-tuple-element.23), channel_id=1, source_target_pairs={{0,2},{2,4},{4,6},{1,3},{3,5},{5,7},{8,10},{10,12},{12,14},{9,11},... | collective-permute-start | bytes 1572872 | tf_op jit(solution)/shard_map/ppermute | solution.py:20
  740.1 4.3 collective-permute-start.14
  741.6 7.2 collective-permute-start.15
  753.7 8.7 %copy-start.5 = (bf16[32,128,256]{2,1,0:T(8,128)(2,1)S(1)}, bf16[32,128,256]{2,1,0:T(8,128)(2,1)}, u32[]{:S(2)}) copy-start(bf16[32,128,256]{2,1,0:T(8,128)(2,1)} %get-tuple-element.5) | copy-start | bytes 6291460
Sparse Core Ops, SparseCore 0:
  33.8 430.6 all-reduce.6
where the time goes:
time: 836 us; the launch traced here: 835 us
  waiting for transfers between devices  446 us (53%)
  other arithmetic  312 us (37%)
  starting transfers between devices  32.6 us (4%)
  between operations  30.1 us (4%)
  local copies, waits for them, and re-layouts  14.6 us (2%)
    psum x1, waiting for transfers between devices, spread(): return lax.psum(kept, axis)  395 us
    sub x4, other arithmetic, shards(): 2.0 * current - previous + courant[None] * laplace - scaled * source[None]  253 us
    concatenate x10, other arithmetic, with_halo(): block = jnp.concatenate([low, block, high], axis=dim)  48.7 us
    ppermute x8, waiting for transfers between devices, with_halo(): lax.ppermute(lax.slice_in_dim(block, block.shape[dim] - width, None, axis...  34 us
    ppermute x8, starting transfers between devices, with_halo(): lax.ppermute(lax.slice_in_dim(block, 0, width, axis=dim), axis, backward)  17.5 us
    ppermute x8, waiting for transfers between devices, with_halo(): lax.ppermute(lax.slice_in_dim(block, 0, width, axis=dim), axis, backward)  16.8 us
  transfers between devices with their start and end apart: 17, of which 16 were waited for; matrix products, arithmetic and copies ran while one was open for 2% of the time, Pallas kernels for 0%

commit v1 on v0

--- a/solution.py
+++ b/solution.py
@@ -7,9 +7,15 @@
 COEFFS = (-205.0 / 72.0, 8.0 / 5.0, -1.0 / 5.0, 8.0 / 315.0, -1.0 / 560.0)
 
 
+def summed_here(x, axis):
+    pieces = lax.all_gather(x, axis, axis=0, tiled=False)
+    total = pieces.sum(axis=0)
+    return total
+
+
 def spread(value, axis, source):
     kept = jnp.where(lax.axis_index(axis) == source, value, 0).astype(value.dtype)
-    return lax.psum(kept, axis)
+    return summed_here(kept, axis)
 
 
 def with_halo(block, sides, width):

time: 836 us -> 1030 us (1.23)
  waiting for transfers between devices: 446 us -> 577 us
  other arithmetic: 312 us -> 365 us
    all_gather x0 -> x6, waiting for transfers between devices: none -> 540 us  [summed_here(): pieces = lax.all_gather(x, axis, axis=0, tiled=False)]
    psum x1 -> x0, waiting for transfers between devices: 395 us -> none  [spread(): return lax.psum(kept, axis)]
    reduce_sum x0 -> x6, other arithmetic: none -> 39.7 us  [summed_here(): total = pieces.sum(axis=0)]
    ppermute x8, waiting for transfers between devices: 34 us -> 20.7 us  [with_halo(): lax.ppermute(lax.slice_in_dim(block, block.shape[dim] - width, None, axis...]
  transfers between devices with their start and end apart: 17 -> 22, of which waited for: 16 -> 14; matrix products, arithmetic and copies ran while one was open for 2% -> 28% of each run, Pallas kernels for 0% -> 0%
where the time goes in v1:
time: 1030 us
  waiting for transfers between devices  577 us (56%)
  other arithmetic  365 us (35%)
  starting transfers between devices  41.3 us (4%)
  between operations  30.7 us (3%)
  local copies, waits for them, and re-layouts  14.6 us (1%)
    all_gather x6, waiting for transfers between devices, summed_here(): pieces = lax.all_gather(x, axis, axis=0, tiled=False)  540 us
    sub x4, other arithmetic, shards(): 2.0 * current - previous + courant[None] * laplace - scaled * source[None]  255 us
    concatenate x10, other arithmetic, with_halo(): block = jnp.concatenate([low, block, high], axis=dim)  59 us
    reduce_sum x6, other arithmetic, summed_here(): total = pieces.sum(axis=0)  39.7 us
    ppermute x8, starting transfers between devices, with_halo(): lax.ppermute(lax.slice_in_dim(block, 0, width, axis=dim), axis, backward)  27.2 us
    ppermute x8, waiting for transfers between devices, with_halo(): lax.ppermute(lax.slice_in_dim(block, block.shape[dim] - width, None, axis...  20.7 us
  transfers between devices with their start and end apart: 22, of which 14 were waited for; matrix products, arithmetic and copies ran while one was open for 28% of the time, Pallas kernels for 0%

profile of v1, /device:TPU:6, one launch (start us, length us, event | category | flops | bytes accessed | tf_op | source)
XLA Modules:
  0.0 1028.0 jit_solution(13175628013835229993)
XLA Ops:
  24.3 9.9 dynamic-slice_select_fusion
  43.8 4.9 collective-permute-done.1
  49.6 7.1 constant_dynamic-update-slice_fusion.1
  67.3 5.7 select_maximum_fusion.12
  73.0 112.2 %all-gather.11.cloned.1.call-done = bf16[4,32,128,256]{3,2,1,0:T(8,128)(2,1)} async-done(((bf16[1,32,128,256]{3,2,1,0:T(8,128)(2,1)}), bf16[4,32,128,256]{3,2,1,0:T(8,128)(2,1)}) %all-gather.11.cloned.1.call-update) | async-done | bytes 8388624 | tf_op jit(solution)/shard_map/all_gather | solution.py:11
  185.2 6.9 reduce_sum.84
  192.1 142.6 %all-gather.9.cloned.1.call-done = bf16[4,32,128,256]{3,2,1,0:T(8,128)(2,1)} async-done(((bf16[1,32,128,256]{3,2,1,0:T(8,128)(2,1)}), bf16[4,32,128,256]{3,2,1,0:T(8,128)(2,1)}) %all-gather.9.cloned.1.call-update) | async-done | bytes 8388624 | tf_op jit(solution)/shard_map/all_gather | solution.py:11
  334.7 6.9 reduce_sum.83
  341.6 142.5 %all-gather.7.cloned.1.call-done = bf16[4,32,128,256]{3,2,1,0:T(8,128)(2,1)} async-done(((bf16[1,32,128,256]{3,2,1,0:T(8,128)(2,1)}), bf16[4,32,128,256]{3,2,1,0:T(8,128)(2,1)}) %all-gather.7.cloned.1.call-update) | async-done | bytes 8388624 | tf_op jit(solution)/shard_map/all_gather | solution.py:11
  484.1 5.2 reduce_sum.82
  489.3 56.5 %fusion.103 = f32[1,32,128,256]{3,2,1,0:T(8,128)S(1)} fusion(f32[1,40,128,256]{3,2,1,0:T(8,128)} %copy-done.5, f32[1,40,4,256]{3,2,1,0:T(4,128)S(1)} %collective-permute-done.3, f32[1,40,4,256]{3,2,1,0:T(4,128)S(1)} %collective-permute-done.2, f32[1,40,136,264]{3,2,1,0:T(8,128)} %select_maximum_fusion.12, f32[1,36,128,256]{3,2,1,0:T(8,128)} %get-tuple-element.29, ...), kind=kLoop, calls=%fused_computation.183 | loop fusion | flops 52428800 | bytes 99942400 | tf_op jit(solution)/shard_map/sub | solution.py:88
  550.3 4.4 collective-permute-done.4
  560.7 5.1 collective-permute-start.6
  565.8 68.3 %all-gather.13.cloned.1.call-done = bf16[4,32,128,256]{3,2,1,0:T(8,128)(2,1)} async-done(((bf16[1,32,128,256]{3,2,1,0:T(8,128)(2,1)}), bf16[4,32,128,256]{3,2,1,0:T(8,128)(2,1)}) %all-gather.13.cloned.1.call-update) | async-done | bytes 8388624 | tf_op jit(solution)/shard_map/all_gather | solution.py:11
  634.0 6.9 reduce_sum.85
  641.0 11.3 %select_maximum_fusion.8 = f32[1,40,136,264]{3,2,1,0:T(8,128)} fusion(f32[1,40,4,256]{3,2,1,0:T(4,128)S(1)} %collective-permute-done.6, f32[1,40,4,256]{3,2,1,0:T(4,128)S(1)} %collective-permute-done.7, f32[1,4,128,256]{3,2,1,0:T(8,128)S(1)} %collective-permute-done.4, f32[1,32,128,256]{3,2,1,0:T(8,128)} %copy-done, ...), kind=kLoop, calls=%fused_computation.16 | loop fusion | flops 17233920 | bytes 11315200 | tf_op jit(solution)/shard_map/concatenate | solution.py:30
  652.3 4.8 pad_maximum_fusion
  657.1 66.1 %fusion.74 = f32[1,32,128,256]{3,2,1,0:T(8,128)} fusion(f32[1,32,128,256]{3,2,1,0:T(8,128)} %copy-done, f32[1,4,128,256]{3,2,1,0:T(8,128)S(1)} %collective-permute-done.5, f32[1,4,128,256]{3,2,1,0:T(8,128)S(1)} %collective-permute-done.4, f32[1,40,136,264]{3,2,1,0:T(8,128)} %select_maximum_fusion.8, f32[1,40,132,256]{3,2,1,0:T(8,128)} %get-tuple-element.11, ...), kind=kLoop, calls=%fused_computation.154 | loop fusion | flops 52428800 | bytes 95420416 | tf_op jit(solution)/shard_map/sub | solution.py:88
  728.8 4.4 collective-permute-done.8
  740.2 4.7 collective-permute-start.10
  744.9 38.5 %all-gather.15.cloned.1.call-done = bf16[4,32,128,256]{3,2,1,0:T(8,128)(2,1)} async-done(((bf16[1,32,128,256]{3,2,1,0:T(8,128)(2,1)}), bf16[4,32,128,256]{3,2,1,0:T(8,128)(2,1)}) %all-gather.15.cloned.1.call-update) | async-done | bytes 8388624 | tf_op jit(solution)/shard_map/all_gather | solution.py:11
  783.3 6.9 reduce_sum.86
  790.2 8.7 pad_maximum_fusion.1
  799.1 8.7 select_maximum_fusion.4
  807.8 67.4 %fusion.43 = f32[1,32,128,256]{3,2,1,0:T(8,128)} fusion(f32[1,32,128,256]{3,2,1,0:T(8,128)} %fusion.74, f32[1,4,128,256]{3,2,1,0:T(8,128)S(1)} %collective-permute-done.9, f32[1,4,128,256]{3,2,1,0:T(8,128)S(1)} %collective-permute-done.8, f32[1,40,136,264]{3,2,1,0:T(8,128)} %select_maximum_fusion.4, f32[1,40,132,256]{3,2,1,0:T(8,128)} %get-tuple-element.7, ...), kind=kLoop, calls=%fused_computation.123 | loop fusion | flops 52428800 | bytes 95420416 | tf_op jit(solution)/shard_map/sub | solution.py:88
  880.9 4.6 collective-permute-done.12
  891.8 4.8 collective-permute-start.14
  896.6 36.1 %all-gather.17.cloned.1.call-done = bf16[4,32,128,256]{3,2,1,0:T(8,128)(2,1)} async-done(((bf16[1,32,128,256]{3,2,1,0:T(8,128)(2,1)}), bf16[4,32,128,256]{3,2,1,0:T(8,128)(2,1)}) %all-gather.17.cloned.1.call-update) | async-done | bytes 8388624 | tf_op jit(solution)/shard_map/all_gather | solution.py:11
  932.7 6.9 reduce_sum.87
  939.6 11.2 %select_maximum_fusion = f32[1,40,136,264]{3,2,1,0:T(8,128)} fusion(f32[1,40,4,256]{3,2,1,0:T(4,128)S(1)} %collective-permute-done.14, f32[1,40,4,256]{3,2,1,0:T(4,128)S(1)} %collective-permute-done.15, f32[1,4,128,256]{3,2,1,0:T(8,128)S(1)} %collective-permute-done.12, f32[1,32,128,256]{3,2,1,0:T(8,128)} %fusion.43, ...), kind=kLoop, calls=%fused_computation.8 | loop fusion | flops 17233920 | bytes 11315200 | tf_op jit(solution)/shard_map/concatenate | solution.py:30
  950.7 4.8 pad_maximum_fusion.2
  955.6 65.3 %fusion.12 = f32[1,32,128,256]{3,2,1,0:T(8,128)} fusion(f32[1,32,128,256]{3,2,1,0:T(8,128)} %fusion.43, f32[1,4,128,256]{3,2,1,0:T(8,128)S(1)} %collective-permute-done.13, f32[1,4,128,256]{3,2,1,0:T(8,128)S(1)} %collective-permute-done.12, f32[1,40,136,264]{3,2,1,0:T(8,128)} %select_maximum_fusion, f32[1,40,132,256]{3,2,1,0:T(8,128)} %get-tuple-element.3, ...), kind=kLoop, calls=%fused_computation.92 | loop fusion | flops 52428800 | bytes 95420416 | tf_op jit(solution)/shard_map/sub | solution.py:88
  (63 shorter events, 56.8 us)
Async XLA Ops:
  7.2 178.0 %all-gather.11.cloned.1.call-start = ((), (), s32[]{:S(2)}) async-start(), calls=%async_computation.2 | async-start | bytes 10485760 | tf_op jit(solution)/shard_map/all_gather | solution.py:11
  34.2 300.4 %all-gather.9.cloned.1.call-start = ((), (), s32[]{:S(2)}) async-start(), calls=%async_computation.1 | async-start | bytes 10485760 | tf_op jit(solution)/shard_map/all_gather | solution.py:11
  35.0 449.2 %all-gather.7.cloned.1.call-start = ((), (), s32[]{:S(2)}) async-start(), calls=%async_computation | async-start | bytes 10485760 | tf_op jit(solution)/shard_map/all_gather | solution.py:11
  35.7 598.3 %all-gather.13.cloned.1.call-start = ((), (), s32[]{:S(2)}) async-start(), calls=%async_computation.3 | async-start | bytes 10485760 | tf_op jit(solution)/shard_map/all_gather | solution.py:11
  36.3 747.1 %all-gather.15.cloned.1.call-start = ((), (), s32[]{:S(2)}) async-start(), calls=%async_computation.4 | async-start | bytes 10485760 | tf_op jit(solution)/shard_map/all_gather | solution.py:11
  36.9 895.8 %all-gather.17.cloned.1.call-start = ((), (), s32[]{:S(2)}) async-start(), calls=%async_computation.5 | async-start | bytes 10485760 | tf_op jit(solution)/shard_map/all_gather | solution.py:11
  38.2 10.5 %collective-permute-start.1 = (f32[1,4,128,256]{3,2,1,0:T(8,128)S(1)}, f32[1,4,128,256]{3,2,1,0:T(8,128)S(1)}, u32[]{:S(2)}, u32[]{:S(2)}) collective-permute-start(f32[1,4,128,256]{3,2,1,0:T(8,128)S(1)} %get-tuple-element.32), channel_id=1, source_target_pairs={{0,2},{2,4},{4,6},{1,3},{3,5},{5,7},{8,10},{10,12},{12,14},{9,11},... | collective-permute-start | bytes 1572872 | tf_op jit(solution)/shard_map/ppermute | solution.py:26
  40.1 16.6 %collective-permute-start = (f32[1,4,128,256]{3,2,1,0:T(8,128)S(1)}, f32[1,4,128,256]{3,2,1,0:T(8,128)S(1)}, u32[]{:S(2)}, u32[]{:S(2)}) collective-permute-start(f32[1,4,128,256]{3,2,1,0:T(8,128)S(1)} %get-tuple-element.31), channel_id=1, source_target_pairs={{2,0},{4,2},{6,4},{3,1},{5,3},{7,5},{10,8},{12,10},{14,12},{11,9},... | collective-permute-start | bytes 1572872 | tf_op jit(solution)/shard_map/ppermute | solution.py:29
  49.6 12.8 %copy-start.6 = (f32[256]{0:T(256)S(1)}, f32[256]{0:T(256)}, u32[]{:S(2)}) copy-start(f32[256]{0:T(256)} %param.14) | copy-start | bytes 3076
  57.6 9.7 copy-start.5
  57.7 5.4 collective-permute-start.2
  60.1 7.2 collective-permute-start.3
  545.8 12.7 %copy-start = (f32[1,32,128,256]{3,2,1,0:T(8,128)}, f32[1,32,128,256]{3,2,1,0:T(8,128)S(1)}, u32[]{:S(2)}) copy-start(f32[1,32,128,256]{3,2,1,0:T(8,128)S(1)} %fusion.103) | copy-start | bytes 12582916
  545.9 8.8 collective-permute-start.4
  548.1 10.5 %collective-permute-start.5 = (f32[1,4,128,256]{3,2,1,0:T(8,128)S(1)}, f32[1,4,128,256]{3,2,1,0:T(8,128)S(1)}, u32[]{:S(2)}, u32[]{:S(2)}) collective-permute-start(f32[1,4,128,256]{3,2,1,0:T(8,128)S(1)} %get-tuple-element.27), channel_id=1, source_target_pairs={{0,2},{2,4},{4,6},{1,3},{3,5},{5,7},{8,10},{10,12},{12,14},{9,11},... | collective-permute-start | bytes 1572872 | tf_op jit(solution)/shard_map/ppermute | solution.py:26
  559.4 81.6 %collective-permute-start.7 = (f32[1,40,4,256]{3,2,1,0:T(4,128)}, f32[1,40,4,256]{3,2,1,0:T(4,128)S(1)}, u32[]{:S(2)}, u32[]{:S(2)}) collective-permute-start(f32[1,40,4,256]{3,2,1,0:T(4,128)} %get-tuple-element.12), channel_id=1, source_target_pairs={{0,1},{2,3},{4,5},{6,7},{8,9},{10,11},{12,13},{14,15},{16,17},{18,... | collective-permute-start | bytes 491528 | tf_op jit(solution)/shard_map/ppermute | solution.py:26
  560.7 80.3 %collective-permute-start.6 = (f32[1,40,4,256]{3,2,1,0:T(4,128)}, f32[1,40,4,256]{3,2,1,0:T(4,128)S(1)}, u32[]{:S(2)}, u32[]{:S(2)}) collective-permute-start(f32[1,40,4,256]{3,2,1,0:T(4,128)} %get-tuple-element.13), channel_id=1, source_target_pairs={{1,0},{3,2},{5,4},{7,6},{9,8},{11,10},{13,12},{15,14},{17,16},{19,... | collective-permute-start | bytes 491528 | tf_op jit(solution)/shard_map/ppermute | solution.py:29
  641.0 11.3 %copy-start.1 = (f32[1,32,128,256]{3,2,1,0:T(8,128)S(1)}, f32[1,32,128,256]{3,2,1,0:T(8,128)}, u32[]{:S(2)}) copy-start(f32[1,32,128,256]{3,2,1,0:T(8,128)} %copy-done) | copy-start | bytes 12582916
  724.4 8.8 collective-permute-start.8
  726.6 10.5 %collective-permute-start.9 = (f32[1,4,128,256]{3,2,1,0:T(8,128)S(1)}, f32[1,4,128,256]{3,2,1,0:T(8,128)S(1)}, u32[]{:S(2)}, u32[]{:S(2)}) collective-permute-start(f32[1,4,128,256]{3,2,1,0:T(8,128)S(1)} %get-tuple-element.25), channel_id=1, source_target_pairs={{0,2},{2,4},{4,6},{1,3},{3,5},{5,7},{8,10},{10,12},{12,14},{9,11},... | collective-permute-start | bytes 1572872 | tf_op jit(solution)/shard_map/ppermute | solution.py:26
  738.9 51.4 %collective-permute-start.11 = (f32[1,40,4,256]{3,2,1,0:T(4,128)}, f32[1,40,4,256]{3,2,1,0:T(4,128)S(1)}, u32[]{:S(2)}, u32[]{:S(2)}) collective-permute-start(f32[1,40,4,256]{3,2,1,0:T(4,128)} %get-tuple-element.8), channel_id=1, source_target_pairs={{0,1},{2,3},{4,5},{6,7},{8,9},{10,11},{12,13},{14,15},{16,17},{18,... | collective-permute-start | bytes 491528 | tf_op jit(solution)/shard_map/ppermute | solution.py:26
  740.2 50.1 %collective-permute-start.10 = (f32[1,40,4,256]{3,2,1,0:T(4,128)}, f32[1,40,4,256]{3,2,1,0:T(4,128)S(1)}, u32[]{:S(2)}, u32[]{:S(2)}) collective-permute-start(f32[1,40,4,256]{3,2,1,0:T(4,128)} %get-tuple-element.9), channel_id=1, source_target_pairs={{1,0},{3,2},{5,4},{7,6},{9,8},{11,10},{13,12},{15,14},{17,16},{19,... | collective-permute-start | bytes 491528 | tf_op jit(solution)/shard_map/ppermute | solution.py:29
  790.2 8.9 copy-start.2
  876.6 9.0 collective-permute-start.12
  878.9 10.5 %collective-permute-start.13 = (f32[1,4,128,256]{3,2,1,0:T(8,128)S(1)}, f32[1,4,128,256]{3,2,1,0:T(8,128)S(1)}, u32[]{:S(2)}, u32[]{:S(2)}) collective-permute-start(f32[1,4,128,256]{3,2,1,0:T(8,128)S(1)} %get-tuple-element.23), channel_id=1, source_target_pairs={{0,2},{2,4},{4,6},{1,3},{3,5},{5,7},{8,10},{10,12},{12,14},{9,11},... | collective-permute-start | bytes 1572872 | tf_op jit(solution)/shard_map/ppermute | solution.py:26
  890.5 49.1 %collective-permute-start.15 = (f32[1,40,4,256]{3,2,1,0:T(4,128)S(1)}, f32[1,40,4,256]{3,2,1,0:T(4,128)S(1)}, u32[]{:S(2)}, u32[]{:S(2)}) collective-permute-start(f32[1,40,4,256]{3,2,1,0:T(4,128)S(1)} %get-tuple-element.4), channel_id=1, source_target_pairs={{0,1},{2,3},{4,5},{6,7},{8,9},{10,11},{12,13},{14,15},{16,17},{18,... | collective-permute-start | bytes 491528 | tf_op jit(solution)/shard_map/ppermute | solution.py:26
  891.8 47.8 %collective-permute-start.14 = (f32[1,40,4,256]{3,2,1,0:T(4,128)S(1)}, f32[1,40,4,256]{3,2,1,0:T(4,128)S(1)}, u32[]{:S(2)}, u32[]{:S(2)}) collective-permute-start(f32[1,40,4,256]{3,2,1,0:T(4,128)S(1)} %get-tuple-element.5), channel_id=1, source_target_pairs={{1,0},{3,2},{5,4},{7,6},{9,8},{11,10},{13,12},{15,14},{17,16},{19,... | collective-permute-start | bytes 491528 | tf_op jit(solution)/shard_map/ppermute | solution.py:29
  939.5 11.2 %copy-start.3 = (f32[1,32,128,256]{3,2,1,0:T(8,128)S(1)}, f32[1,32,128,256]{3,2,1,0:T(8,128)}, u32[]{:S(2)}) copy-start(f32[1,32,128,256]{3,2,1,0:T(8,128)} %fusion.43) | copy-start | bytes 12582916
  950.7 4.8 copy-start.4
Sparse Core Ops, SparseCore 0:
  34.3 150.8 all-gather.10
  186.8 147.8 all-gather.8
  336.2 147.8 all-gather.6
  486.1 147.8 all-gather.12
  635.4 147.8 all-gather.14
  784.8 147.8 all-gather.16
